TPU v7x, 32 devices: a whole 2x2x4 slice. The times are simulated.
32 devices in a mesh: blk: 16 (over z, y, core), grp: 2 (over x).
Axes of the slice: x: 2, y: 2, z: 4, core: 2. Of those that a mesh axis runs over, the one named last changes fastest.
Arguments:
- tracers: float32 [2, 16, 128, 256], P(None, None, 'blk', 'grp'), may hold values from -6 to 6
- velocity: float32 [2, 16, 128, 256], P(None, None, 'blk', 'grp'), may hold values from -3 to 3
- depth_levels: int32 [128, 256], P('blk', 'grp'), may hold values from 0 to 16, as said below
- vdiff: float32 [15], replicated, may hold values from 0.05 to 0.45
Outputs:
- new_tracers: float32 [2, 16, 128, 256], P(None, None, 'blk', 'grp')
- surface: float32 [128, 256], P('blk', 'grp')
- residual: float32 [128, 256], P('blk', 'grp')
Inputs may be any that keep to these rules, and one draw needn't show every extreme that they name: `depth_levels`: 16 and 0 are both reached in every draw.
All inputs are finite; a program needn't handle non-finite values.
Results may differ from a plain program's by a relative error of at most 0.0003.
Values sent between devices are 32-bit elements; how exact they have to be, the bound alone decides.
No kernel may reach another device: no remote copies, remote signals or barrier semaphores. Data moves between devices by JAX's collectives and lax.ppermute only.
A program may use at most 64 MiB of HBM per device.

v0:
```python
import jax
import jax.numpy as jnp
from jax import lax
from jax.sharding import PartitionSpec as P

ITERS = 3
TIME_STEP = 0.2
MIX_COEF = 0.25
SEA_DIAG = 0.5


def swapped(value, axis, stride):
    return lax.ppermute(value, axis, [(i, i ^ 1 << stride) for i in range(lax.axis_size(axis))])


def padded_2(cells, sides, width, closed):
    for axis, dim in sides:
        count = lax.axis_size(axis)
        ends = count if closed else count - 1
        head = lax.slice_in_dim(cells, 0, width, axis=dim)
        tail = lax.slice_in_dim(cells, cells.shape[dim] - width, cells.shape[dim], axis=dim)
        cells = jnp.concatenate(
            [
                lax.ppermute(tail, axis, [(i, (i + 1) % count) for i in range(ends)]),
                cells,
                lax.ppermute(head, axis, [((i + 1) % count, i) for i in range(ends)]),
            ],
            axis=dim,
        )
    return cells


def tracer_step(tracer, velocity, depth_pad, vdiff):
    count = tracer.shape[1]
    levels = jnp.arange(count, dtype=jnp.float32)[:, None, None]
    wet_mask = (levels < depth_pad[None]).astype(jnp.float32)
    east_vel = velocity[0]
    north_vel = velocity[1]
    row_set = tracer[:, :, 1:-1, :]
    wet_rows = wet_mask[:, 1:-1, :]
    east_rows = east_vel[:, 1:-1, :]
    east_open = wet_rows[:, :, :-1] * wet_rows[:, :, 1:]
    east_face = 0.5 * (east_rows[:, :, :-1] + east_rows[:, :, 1:])
    east_flux = east_open * (
        east_face * 0.5 * (row_set[..., :-1] + row_set[..., 1:])
        - MIX_COEF * (row_set[..., 1:] - row_set[..., :-1])
    )
    col_set = tracer[:, :, :, 1:-1]
    wet_cols = wet_mask[:, :, 1:-1]
    north_cols = north_vel[:, :, 1:-1]
    north_open = wet_cols[:, :-1, :] * wet_cols[:, 1:, :]
    north_face = 0.5 * (north_cols[:, :-1, :] + north_cols[:, 1:, :])
    north_flux = north_open * (
        north_face * 0.5 * (col_set[:, :, :-1, :] + col_set[:, :, 1:, :])
        - MIX_COEF * (col_set[:, :, 1:, :] - col_set[:, :, :-1, :])
    )
    centre = tracer[:, :, 1:-1, 1:-1]
    wet_centre = wet_mask[:, 1:-1, 1:-1]
    vert_open = wet_centre[:-1] * wet_centre[1:]
    vert_flux = vdiff[:, None, None] * vert_open * (centre[:, 1:] - centre[:, :-1])
    border = jnp.zeros_like(centre[:, :1])
    vert_flux = jnp.concatenate([border, vert_flux, border], 1)
    tendency = (
        vert_flux[:, 1:]
        - vert_flux[:, :-1]
        - (east_flux[..., 1:] - east_flux[..., :-1])
        - (north_flux[:, :, 1:, :] - north_flux[:, :, :-1, :])
    )
    return wet_centre * (centre + TIME_STEP * tendency)


def column_forcing(velocity, depth_pad):
    count = velocity.shape[1]
    levels = jnp.arange(count, dtype=jnp.float32)[:, None, None]
    wet_mask = (levels < depth_pad[None]).astype(jnp.float32)
    east_sum = jnp.sum(wet_mask * velocity[0], 0)
    north_sum = jnp.sum(wet_mask * velocity[1], 0)
    ocean_mask = (depth_pad[1:-1, 1:-1] > 0).astype(jnp.float32)
    return ocean_mask * (
        0.5 * (east_sum[1:-1, 2:] - east_sum[1:-1, :-2])
        + 0.5 * (north_sum[2:, 1:-1] - north_sum[:-2, 1:-1])
    )


def sea_operator(field_pad, depth_pad, count):
    centre = field_pad[1:-1, 1:-1]
    depth_c = depth_pad[1:-1, 1:-1]
    ocean_mask = (depth_c > 0).astype(jnp.float32)
    total = SEA_DIAG * centre
    for rows_at, cols_at in (
        (slice(1, -1), slice(2, None)),
        (slice(1, -1), slice(None, -2)),
        (slice(2, None), slice(1, -1)),
        (slice(None, -2), slice(1, -1)),
    ):
        weight = jnp.minimum(depth_c, depth_pad[rows_at, cols_at]) / count
        total = total + weight * (centre - field_pad[rows_at, cols_at])
    return ocean_mask * total + (1.0 - ocean_mask) * centre


def extend(fields, fold_sign):
    top_row = fields[:, -1, :]
    partner = top_row
    for bit_index in range(lax.axis_size("grp").bit_length() - 1):
        partner = swapped(partner, "grp", bit_index)
    mirror = partner[:, ::-1]
    northmost = lax.axis_index("blk") == lax.axis_size("blk") - 1
    row_halo = padded_2(fields, (("blk", 1),), 1, False)
    north_row = jnp.where(northmost, mirror * fold_sign[:, None], row_halo[:, -1, :])
    grown = jnp.concatenate([row_halo[:, :-1, :], north_row[:, None, :]], 1)
    return padded_2(grown, (("grp", 2),), 1, True)


def two_sums(residual, applied):
    return lax.psum((jnp.sum(residual * residual), jnp.sum(residual * applied)), ("blk", "grp"))


def shards(tracers, velocity, depth_levels, vdiff):
    count = tracers.shape[1]
    height, breadth = depth_levels.shape
    fields = jnp.concatenate(
        [
            tracers.reshape(2 * count, height, breadth),
            velocity.reshape(2 * count, height, breadth),
            depth_levels.astype(jnp.float32)[None],
        ],
        0,
    )
    fold_sign = jnp.concatenate(
        [
            jnp.ones((2 * count,), jnp.float32),
            -jnp.ones((2 * count,), jnp.float32),
            jnp.ones((1,), jnp.float32),
        ]
    )
    padded = extend(fields, fold_sign)
    tracer_pad = padded[: 2 * count].reshape(2, count, height + 2, breadth + 2)
    velocity_pad = padded[2 * count : 4 * count].reshape(2, count, height + 2, breadth + 2)
    depth_pad = padded[4 * count]
    new_tracers = tracer_step(tracer_pad, velocity_pad, depth_pad, vdiff)
    forcing = column_forcing(velocity_pad, depth_pad)

    def apply_op(field):
        grown = extend(field[None], jnp.ones((1,), jnp.float32))[0]
        return sea_operator(grown, depth_pad, count)

    surface = jnp.zeros_like(forcing)
    residual = forcing
    applied = apply_op(residual)
    norm_now, product = two_sums(residual, applied)
    step_len = norm_now / product
    direction, along = (residual, applied)
    for sweep in range(ITERS):
        surface = surface + step_len * direction
        residual = residual - step_len * along
        if sweep + 1 < ITERS:
            applied = apply_op(residual)
            norm_next, product = two_sums(residual, applied)
            beta_ratio = norm_next / norm_now
            step_len = norm_next / (product - beta_ratio * norm_next / step_len)
            direction = residual + beta_ratio * direction
            along = applied + beta_ratio * along
            norm_now = norm_next
    return (new_tracers, surface, residual)


def solution(mesh):
    return jax.shard_map(
        shards,
        mesh=mesh,
        in_specs=(P(None, None, "blk", "grp"), P(None, None, "blk", "grp"), P("blk", "grp"), P()),
        out_specs=(P(None, None, "blk", "grp"), P("blk", "grp"), P("blk", "grp")),
        check_vma=False,
    )
```

profile of v0, /device:TPU:0, one launch (start us, length us, event | category | flops | bytes accessed | tf_op | source)
XLA Modules:
  0.0 197.3 jit_solution(13682118741915809105)
XLA Ops:
  2.5 3.0 %collective-permute-start.1 = (f32[65,128]{1,0:T(8,128)S(1)}, f32[65,128]{1,0:T(8,128)S(1)}, u32[]{:S(2)}, u32[]{:S(2)}) collective-permute-start(f32[65,128]{1,0:T(8,128)S(1)} %bitcast.70), channel_id=1, source_target_pairs={{0,1},{1,0},{2,3},{3,2},{4,5},{5,4},{6,7},{7,6},{8,9},{9,8},{10,11... | collective-permute-start | bytes 99848 | tf_op jit(solution)/shard_map/ppermute | solution.py:13
  5.5 1.3 collective-permute-start.2
  6.8 3.0 %collective-permute-start = (f32[65,1,128]{2,1,0:T(1,128)S(1)}, f32[65,1,128]{2,1,0:T(1,128)S(1)}, u32[]{:S(2)}, u32[]{:S(2)}) collective-permute-start(f32[65,1,128]{2,1,0:T(1,128)S(1)} %get-tuple-element.27), channel_id=1, source_target_pairs={{0,2},{2,4},{4,6},{6,8},{8,10},{10,12},{12,14},{14,16},{16,18},{18... | collective-permute-start | bytes 99848 | tf_op jit(solution)/shard_map/ppermute | solution.py:24
  12.5 2.0 %collective-permute-start.3 = (f32[65,10,1]{0,2,1:T(1,128)S(1)}, f32[65,10,1]{0,2,1:T(1,128)S(1)}, u32[]{:S(2)}, u32[]{:S(2)}) collective-permute-start(f32[65,10,1]{0,2,1:T(1,128)S(1)} %copy.30), channel_id=1, source_target_pairs={{0,1},{1,0},{2,3},{3,2},{4,5},{5,4},{6,7},{7,6},{8,9},{9,8},{10,11... | collective-permute-start | bytes 7808 | tf_op jit(solution)/shard_map/ppermute | solution.py:24
  14.6 1.6 collective-permute-done.3
  17.8 2.2 %collective-permute-start.5 = (f32[1,1,128]{2,1,0:T(1,128)S(1)}, f32[1,1,128]{2,1,0:T(1,128)S(1)}, u32[]{:S(2)}, u32[]{:S(2)}) collective-permute-start(f32[1,1,128]{2,1,0:T(1,128)S(1)} %get-tuple-element.43), channel_id=1, source_target_pairs={{0,2},{2,4},{4,6},{6,8},{8,10},{10,12},{12,14},{14,16},{16,18},{18... | collective-permute-start | bytes 1544 | tf_op jit(solution)/shard_map/ppermute | solution.py:24
  19.9 1.9 collective-permute-start.6
  21.8 1.3 collective-permute-start.7
  25.2 2.3 %collective-permute-done.7 = f32[1,1,128]{2,1,0:T(1,128)S(1)} collective-permute-done((f32[1,1,128]{2,1,0:T(1,128)S(1)}, f32[1,1,128]{2,1,0:T(1,128)S(1)}, u32[]{:S(2)}, u32[]{:S(2)}) %collective-permute-start.7) | collective-permute-done | bytes 544 | tf_op jit(solution)/shard_map/ppermute | solution.py:26
  28.2 1.5 collective-permute-start.9
  29.6 1.6 collective-permute-done.8
  32.6 43.7 %all-reduce.4 = (f32[]{:T(128)}, f32[]{:T(128)}) all-reduce(f32[]{:T(128)} %get-tuple-element.13, f32[]{:T(128)} %get-tuple-element.12), channel_id=1, replica_groups=mesh['blk'=16,'grp'=2] {'blk','grp'}, use_global_device_ids=true, to_apply=%region_3.4 | all-reduce | flops 2 | bytes 16 | tf_op jit(solution)/shard_map/psum | solution.py:115
  77.6 2.3 %collective-permute-start.11 = (f32[1,128]{1,0:T(1,128)S(1)}, f32[1,128]{1,0:T(1,128)S(1)}, u32[]{:S(2)}, u32[]{:S(2)}) collective-permute-start(f32[1,128]{1,0:T(1,128)S(1)} %get-tuple-element.41), channel_id=1, source_target_pairs={{0,1},{1,0},{2,3},{3,2},{4,5},{5,4},{6,7},{7,6},{8,9},{9,8},{10,11... | collective-permute-start | bytes 1544 | tf_op jit(solution)/shard_map/ppermute | solution.py:13
  80.0 1.3 collective-permute-start.12
  81.5 3.0 %collective-permute-start.10 = (f32[1,1,128]{2,1,0:T(1,128)S(1)}, f32[1,1,128]{2,1,0:T(1,128)S(1)}, u32[]{:S(2)}, u32[]{:S(2)}) collective-permute-start(f32[1,1,128]{2,1,0:T(1,128)S(1)} %get-tuple-element.40), channel_id=1, source_target_pairs={{0,2},{2,4},{4,6},{6,8},{8,10},{10,12},{12,14},{14,16},{16,18},{18... | collective-permute-start | bytes 1544 | tf_op jit(solution)/shard_map/ppermute | solution.py:24
  85.5 2.0 %collective-permute-start.14 = (f32[1,10,1]{2,1,0:T(8,128)S(1)}, f32[1,10,1]{2,1,0:T(8,128)S(1)}, u32[]{:S(2)}, u32[]{:S(2)}) collective-permute-start(f32[1,10,1]{2,1,0:T(8,128)S(1)} %get-tuple-element.32), channel_id=1, source_target_pairs={{1,0},{0,1},{3,2},{2,3},{5,4},{4,5},{7,6},{6,7},{9,8},{8,9},{11,10... | collective-permute-start | bytes 128 | tf_op jit(solution)/shard_map/ppermute | solution.py:26
  87.5 1.6 collective-permute-done.13
  89.9 42.7 %all-reduce.3 = (f32[]{:T(128)}, f32[]{:T(128)}) all-reduce(f32[]{:T(128)} %get-tuple-element.11, f32[]{:T(128)} %get-tuple-element.10), channel_id=1, replica_groups=mesh['blk'=16,'grp'=2] {'blk','grp'}, use_global_device_ids=true, to_apply=%region_7.8 | all-reduce | flops 2 | bytes 16 | tf_op jit(solution)/shard_map/psum | solution.py:115
  137.4 2.3 %collective-permute-start.16 = (f32[1,128]{1,0:T(1,128)S(1)}, f32[1,128]{1,0:T(1,128)S(1)}, u32[]{:S(2)}, u32[]{:S(2)}) collective-permute-start(f32[1,128]{1,0:T(1,128)S(1)} %get-tuple-element.38), channel_id=1, source_target_pairs={{0,1},{1,0},{2,3},{3,2},{4,5},{5,4},{6,7},{7,6},{8,9},{9,8},{10,11... | collective-permute-start | bytes 1544 | tf_op jit(solution)/shard_map/ppermute | solution.py:13
  139.7 1.3 collective-permute-start.17
  141.9 3.0 %collective-permute-start.15 = (f32[1,1,128]{2,1,0:T(1,128)S(1)}, f32[1,1,128]{2,1,0:T(1,128)S(1)}, u32[]{:S(2)}, u32[]{:S(2)}) collective-permute-start(f32[1,1,128]{2,1,0:T(1,128)S(1)} %get-tuple-element.37), channel_id=1, source_target_pairs={{0,2},{2,4},{4,6},{6,8},{8,10},{10,12},{12,14},{14,16},{16,18},{18... | collective-permute-start | bytes 1544 | tf_op jit(solution)/shard_map/ppermute | solution.py:24
  145.8 2.0 %collective-permute-start.19 = (f32[1,10,1]{2,1,0:T(8,128)S(1)}, f32[1,10,1]{2,1,0:T(8,128)S(1)}, u32[]{:S(2)}, u32[]{:S(2)}) collective-permute-start(f32[1,10,1]{2,1,0:T(8,128)S(1)} %get-tuple-element.30), channel_id=1, source_target_pairs={{1,0},{0,1},{3,2},{2,3},{5,4},{4,5},{7,6},{6,7},{9,8},{8,9},{11,10... | collective-permute-start | bytes 128 | tf_op jit(solution)/shard_map/ppermute | solution.py:26
  147.8 1.6 collective-permute-done.18
  150.4 42.3 %all-reduce.2 = (f32[]{:T(128)}, f32[]{:T(128)}) all-reduce(f32[]{:T(128)} %get-tuple-element.9, f32[]{:T(128)} %get-tuple-element.8), channel_id=1, replica_groups=mesh['blk'=16,'grp'=2] {'blk','grp'}, use_global_device_ids=true, to_apply=%region_11.12 | all-reduce | flops 2 | bytes 16 | tf_op jit(solution)/shard_map/psum | solution.py:115
  (86 shorter events, 15.3 us)
Async XLA Ops:
  2.5 7.4 %collective-permute-start.1 = (f32[65,128]{1,0:T(8,128)S(1)}, f32[65,128]{1,0:T(8,128)S(1)}, u32[]{:S(2)}, u32[]{:S(2)}) collective-permute-start(f32[65,128]{1,0:T(8,128)S(1)} %bitcast.70), channel_id=1, source_target_pairs={{0,1},{1,0},{2,3},{3,2},{4,5},{5,4},{6,7},{7,6},{8,9},{9,8},{10,11... | collective-permute-start | bytes 99848 | tf_op jit(solution)/shard_map/ppermute | solution.py:13
  5.5 4.4 %collective-permute-start.2 = (f32[65,1,128]{2,0,1:T(8,128)S(1)}, f32[65,1,128]{2,0,1:T(8,128)S(1)}, u32[]{:S(2)}, u32[]{:S(2)}) collective-permute-start(f32[65,1,128]{2,0,1:T(8,128)S(1)} %copy.46), channel_id=1, source_target_pairs={{2,0},{4,2},{6,4},{8,6},{10,8},{12,10},{14,12},{16,14},{18,16},{20... | collective-permute-start | bytes 99848 | tf_op jit(solution)/shard_map/ppermute | solution.py:26
  6.8 3.9 %collective-permute-start = (f32[65,1,128]{2,1,0:T(1,128)S(1)}, f32[65,1,128]{2,1,0:T(1,128)S(1)}, u32[]{:S(2)}, u32[]{:S(2)}) collective-permute-start(f32[65,1,128]{2,1,0:T(1,128)S(1)} %get-tuple-element.27), channel_id=1, source_target_pairs={{0,2},{2,4},{4,6},{6,8},{8,10},{10,12},{12,14},{14,16},{16,18},{18... | collective-permute-start | bytes 99848 | tf_op jit(solution)/shard_map/ppermute | solution.py:24
  12.0 2.5 %copy-start = (f32[2,16,8,128]{3,2,1,0:T(8,128)S(1)}, f32[2,16,8,128]{3,2,1,0:T(8,128)}, u32[]{:S(2)}) copy-start(f32[2,16,8,128]{3,2,1,0:T(8,128)} %param.5) | copy-start | bytes 393220
  12.0 2.5 %copy-start.1 = (f32[2,16,8,128]{3,2,1,0:T(8,128)S(1)}, f32[2,16,8,128]{3,2,1,0:T(8,128)}, u32[]{:S(2)}) copy-start(f32[2,16,8,128]{3,2,1,0:T(8,128)} %param.4) | copy-start | bytes 393220
  12.4 4.1 %collective-permute-start.4 = (f32[65,10,1]{0,2,1:T(1,128)S(1)}, f32[65,10,1]{0,2,1:T(1,128)S(1)}, u32[]{:S(2)}, u32[]{:S(2)}) collective-permute-start(f32[65,10,1]{0,2,1:T(1,128)S(1)} %copy.31), channel_id=1, source_target_pairs={{1,0},{0,1},{3,2},{2,3},{5,4},{4,5},{7,6},{6,7},{9,8},{8,9},{11,10... | collective-permute-start | bytes 7808 | tf_op jit(solution)/shard_map/ppermute | solution.py:26
  12.5 3.7 %collective-permute-start.3 = (f32[65,10,1]{0,2,1:T(1,128)S(1)}, f32[65,10,1]{0,2,1:T(1,128)S(1)}, u32[]{:S(2)}, u32[]{:S(2)}) collective-permute-start(f32[65,10,1]{0,2,1:T(1,128)S(1)} %copy.30), channel_id=1, source_target_pairs={{0,1},{1,0},{2,3},{3,2},{4,5},{5,4},{6,7},{7,6},{8,9},{9,8},{10,11... | collective-permute-start | bytes 7808 | tf_op jit(solution)/shard_map/ppermute | solution.py:24
  17.8 9.8 %collective-permute-start.5 = (f32[1,1,128]{2,1,0:T(1,128)S(1)}, f32[1,1,128]{2,1,0:T(1,128)S(1)}, u32[]{:S(2)}, u32[]{:S(2)}) collective-permute-start(f32[1,1,128]{2,1,0:T(1,128)S(1)} %get-tuple-element.43), channel_id=1, source_target_pairs={{0,2},{2,4},{4,6},{6,8},{8,10},{10,12},{12,14},{14,16},{16,18},{18... | collective-permute-start | bytes 1544 | tf_op jit(solution)/shard_map/ppermute | solution.py:24
  19.9 5.2 %collective-permute-start.6 = (f32[1,128]{1,0:T(1,128)S(1)}, f32[1,128]{1,0:T(1,128)S(1)}, u32[]{:S(2)}, u32[]{:S(2)}) collective-permute-start(f32[1,128]{1,0:T(1,128)S(1)} %get-tuple-element.44), channel_id=1, source_target_pairs={{0,1},{1,0},{2,3},{3,2},{4,5},{5,4},{6,7},{7,6},{8,9},{9,8},{10,11... | collective-permute-start | bytes 1544 | tf_op jit(solution)/shard_map/ppermute | solution.py:13
  21.8 5.7 %collective-permute-start.7 = (f32[1,1,128]{2,1,0:T(1,128)S(1)}, f32[1,1,128]{2,1,0:T(1,128)S(1)}, u32[]{:S(2)}, u32[]{:S(2)}) collective-permute-start(f32[1,1,128]{2,1,0:T(1,128)S(1)} %get-tuple-element.45), channel_id=1, source_target_pairs={{2,0},{4,2},{6,4},{8,6},{10,8},{12,10},{14,12},{16,14},{18,16},{20... | collective-permute-start | bytes 1544 | tf_op jit(solution)/shard_map/ppermute | solution.py:26
  24.3 0.7 copy-start.2
  27.6 3.7 %collective-permute-start.8 = (f32[1,10,1]{2,1,0:T(8,128)S(1)}, f32[1,10,1]{2,1,0:T(8,128)S(1)}, u32[]{:S(2)}, u32[]{:S(2)}) collective-permute-start(f32[1,10,1]{2,1,0:T(8,128)S(1)} %get-tuple-element.33), channel_id=1, source_target_pairs={{0,1},{1,0},{2,3},{3,2},{4,5},{5,4},{6,7},{7,6},{8,9},{9,8},{10,11... | collective-permute-start | bytes 128 | tf_op jit(solution)/shard_map/ppermute | solution.py:24
  28.2 3.7 %collective-permute-start.9 = (f32[1,10,1]{2,1,0:T(8,128)S(1)}, f32[1,10,1]{2,1,0:T(8,128)S(1)}, u32[]{:S(2)}, u32[]{:S(2)}) collective-permute-start(f32[1,10,1]{2,1,0:T(8,128)S(1)} %get-tuple-element.34), channel_id=1, source_target_pairs={{1,0},{0,1},{3,2},{2,3},{5,4},{4,5},{7,6},{6,7},{9,8},{8,9},{11,10... | collective-permute-start | bytes 128 | tf_op jit(solution)/shard_map/ppermute | solution.py:26
  77.6 6.9 %collective-permute-start.11 = (f32[1,128]{1,0:T(1,128)S(1)}, f32[1,128]{1,0:T(1,128)S(1)}, u32[]{:S(2)}, u32[]{:S(2)}) collective-permute-start(f32[1,128]{1,0:T(1,128)S(1)} %get-tuple-element.41), channel_id=1, source_target_pairs={{0,1},{1,0},{2,3},{3,2},{4,5},{5,4},{6,7},{7,6},{8,9},{9,8},{10,11... | collective-permute-start | bytes 1544 | tf_op jit(solution)/shard_map/ppermute | solution.py:13
  80.0 4.7 %collective-permute-start.12 = (f32[1,1,128]{2,1,0:T(1,128)S(1)}, f32[1,1,128]{2,1,0:T(1,128)S(1)}, u32[]{:S(2)}, u32[]{:S(2)}) collective-permute-start(f32[1,1,128]{2,1,0:T(1,128)S(1)} %get-tuple-element.42), channel_id=1, source_target_pairs={{2,0},{4,2},{6,4},{8,6},{10,8},{12,10},{14,12},{16,14},{18,16},{20... | collective-permute-start | bytes 1544 | tf_op jit(solution)/shard_map/ppermute | solution.py:26
  81.5 3.8 %collective-permute-start.10 = (f32[1,1,128]{2,1,0:T(1,128)S(1)}, f32[1,1,128]{2,1,0:T(1,128)S(1)}, u32[]{:S(2)}, u32[]{:S(2)}) collective-permute-start(f32[1,1,128]{2,1,0:T(1,128)S(1)} %get-tuple-element.40), channel_id=1, source_target_pairs={{0,2},{2,4},{4,6},{6,8},{8,10},{10,12},{12,14},{14,16},{16,18},{18... | collective-permute-start | bytes 1544 | tf_op jit(solution)/shard_map/ppermute | solution.py:24
  85.4 3.7 %collective-permute-start.13 = (f32[1,10,1]{2,1,0:T(8,128)S(1)}, f32[1,10,1]{2,1,0:T(8,128)S(1)}, u32[]{:S(2)}, u32[]{:S(2)}) collective-permute-start(f32[1,10,1]{2,1,0:T(8,128)S(1)} %get-tuple-element.31), channel_id=1, source_target_pairs={{0,1},{1,0},{2,3},{3,2},{4,5},{5,4},{6,7},{7,6},{8,9},{9,8},{10,11... | collective-permute-start | bytes 128 | tf_op jit(solution)/shard_map/ppermute | solution.py:24
  85.5 3.7 %collective-permute-start.14 = (f32[1,10,1]{2,1,0:T(8,128)S(1)}, f32[1,10,1]{2,1,0:T(8,128)S(1)}, u32[]{:S(2)}, u32[]{:S(2)}) collective-permute-start(f32[1,10,1]{2,1,0:T(8,128)S(1)} %get-tuple-element.32), channel_id=1, source_target_pairs={{1,0},{0,1},{3,2},{2,3},{5,4},{4,5},{7,6},{6,7},{9,8},{8,9},{11,10... | collective-permute-start | bytes 128 | tf_op jit(solution)/shard_map/ppermute | solution.py:26
  137.4 7.5 %collective-permute-start.16 = (f32[1,128]{1,0:T(1,128)S(1)}, f32[1,128]{1,0:T(1,128)S(1)}, u32[]{:S(2)}, u32[]{:S(2)}) collective-permute-start(f32[1,128]{1,0:T(1,128)S(1)} %get-tuple-element.38), channel_id=1, source_target_pairs={{0,1},{1,0},{2,3},{3,2},{4,5},{5,4},{6,7},{7,6},{8,9},{9,8},{10,11... | collective-permute-start | bytes 1544 | tf_op jit(solution)/shard_map/ppermute | solution.py:13
  139.7 5.3 %collective-permute-start.17 = (f32[1,1,128]{2,1,0:T(1,128)S(1)}, f32[1,1,128]{2,1,0:T(1,128)S(1)}, u32[]{:S(2)}, u32[]{:S(2)}) collective-permute-start(f32[1,1,128]{2,1,0:T(1,128)S(1)} %get-tuple-element.39), channel_id=1, source_target_pairs={{2,0},{4,2},{6,4},{8,6},{10,8},{12,10},{14,12},{16,14},{18,16},{20... | collective-permute-start | bytes 1544 | tf_op jit(solution)/shard_map/ppermute | solution.py:26
  141.9 3.8 %collective-permute-start.15 = (f32[1,1,128]{2,1,0:T(1,128)S(1)}, f32[1,1,128]{2,1,0:T(1,128)S(1)}, u32[]{:S(2)}, u32[]{:S(2)}) collective-permute-start(f32[1,1,128]{2,1,0:T(1,128)S(1)} %get-tuple-element.37), channel_id=1, source_target_pairs={{0,2},{2,4},{4,6},{6,8},{8,10},{10,12},{12,14},{14,16},{16,18},{18... | collective-permute-start | bytes 1544 | tf_op jit(solution)/shard_map/ppermute | solution.py:24
  145.8 3.7 %collective-permute-start.18 = (f32[1,10,1]{2,1,0:T(8,128)S(1)}, f32[1,10,1]{2,1,0:T(8,128)S(1)}, u32[]{:S(2)}, u32[]{:S(2)}) collective-permute-start(f32[1,10,1]{2,1,0:T(8,128)S(1)} %get-tuple-element.29), channel_id=1, source_target_pairs={{0,1},{1,0},{2,3},{3,2},{4,5},{5,4},{6,7},{7,6},{8,9},{9,8},{10,11... | collective-permute-start | bytes 128 | tf_op jit(solution)/shard_map/ppermute | solution.py:24
  145.8 3.8 %collective-permute-start.19 = (f32[1,10,1]{2,1,0:T(8,128)S(1)}, f32[1,10,1]{2,1,0:T(8,128)S(1)}, u32[]{:S(2)}, u32[]{:S(2)}) collective-permute-start(f32[1,10,1]{2,1,0:T(8,128)S(1)} %get-tuple-element.30), channel_id=1, source_target_pairs={{1,0},{0,1},{3,2},{2,3},{5,4},{4,5},{7,6},{6,7},{9,8},{8,9},{11,10... | collective-permute-start | bytes 128 | tf_op jit(solution)/shard_map/ppermute | solution.py:26
where the time goes:
time: 198 us; the launch traced here: 197 us
  blocking collectives  129 us (65%)
  starting transfers between devices  34.1 us (17%)
  between operations  11.1 us (6%)
  waiting for transfers between devices  10.9 us (6%)
  other arithmetic  9.03 us (5%)
  local copies, waits for them, and re-layouts  3.44 us (2%)
    psum x3, blocking collectives, two_sums(): lax.psum((jnp.sum(residual * residual), jnp.sum(residual * applied)), ('b...  129 us
    ppermute x8, starting transfers between devices, padded_2(): lax.ppermute(tail, axis, [(i, (i + 1) % count) for i in range(ends)])  13.9 us
    ppermute x8, starting transfers between devices, padded_2(): lax.ppermute(head, axis, [((i + 1) % count, i) for i in range(ends)])  10.7 us
    ppermute x4, starting transfers between devices, swapped(): lax.ppermute(value, axis, [(i, i ^ 1 << stride) for i in range(lax.axis_s...  9.6 us
    ppermute x8, waiting for transfers between devices, padded_2(): lax.ppermute(tail, axis, [(i, (i + 1) % count) for i in range(ends)])  7.85 us
  transfers between devices with their start and end apart: 20, of which 10 were waited for; matrix products, arithmetic and copies ran while one was open for 2% of the time, Pallas kernels for 0%

commit v1 on v0

--- a/solution.py
+++ b/solution.py
@@ -7,6 +7,11 @@
 TIME_STEP = 0.2
 MIX_COEF = 0.25
 SEA_DIAG = 0.5
+
+
+def one_after_other(value_2, first, second):
+    half = lax.psum(value_2, first)
+    return lax.psum(half, second)
 
 
 def swapped(value, axis, stride):
@@ -112,7 +117,9 @@
 
 
 def two_sums(residual, applied):
-    return lax.psum((jnp.sum(residual * residual), jnp.sum(residual * applied)), ("blk", "grp"))
+    return one_after_other(
+        (jnp.sum(residual * residual), jnp.sum(residual * applied)), "grp", "blk"
+    )
 
 
 def shards(tracers, velocity, depth_levels, vdiff):

time: 198 us -> 178 us (0.90)
  blocking collectives: 129 us -> 109 us
    psum x3 -> x6, blocking collectives: 129 us -> 109 us  [the longest x3 92.6 us: one_after_other(): return lax.psum(half, second)]
where the time goes in v1:
time: 178 us; the launch traced here: 177 us
  blocking collectives  109 us (61%)
  starting transfers between devices  32.6 us (18%)
  waiting for transfers between devices  11.7 us (7%)
  between operations  10.9 us (6%)
  other arithmetic  9.1 us (5%)
  local copies, waits for them, and re-layouts  3.44 us (2%)
    psum x3, blocking collectives, one_after_other(): return lax.psum(half, second)  92.6 us
    psum x3, blocking collectives, one_after_other(): half = lax.psum(value_2, first)  16.7 us
    ppermute x8, starting transfers between devices, padded_2(): lax.ppermute(tail, axis, [(i, (i + 1) % count) for i in range(ends)])  14.9 us
    ppermute x8, starting transfers between devices, padded_2(): lax.ppermute(head, axis, [((i + 1) % count, i) for i in range(ends)])  9.69 us
    ppermute x4, starting transfers between devices, swapped(): lax.ppermute(value, axis, [(i, i ^ 1 << stride) for i in range(lax.axis_s...  8.06 us
    ppermute x8, waiting for transfers between devices, padded_2(): lax.ppermute(tail, axis, [(i, (i + 1) % count) for i in range(ends)])  7.93 us
    ppermute x8, waiting for transfers between devices, padded_2(): lax.ppermute(head, axis, [((i + 1) % count, i) for i in range(ends)])  3.79 us
  transfers between devices with their start and end apart: 20, of which 10 were waited for; matrix products, arithmetic and copies ran while one was open for 2% of the time, Pallas kernels for 0%

profile of v1, /device:TPU:0, one launch (start us, length us, event | category | flops | bytes accessed | tf_op | source)
XLA Modules:
  0.0 177.0 jit_solution(1138090509801742430)
XLA Ops:
  2.5 3.0 %collective-permute-start.1 = (f32[65,128]{1,0:T(8,128)S(1)}, f32[65,128]{1,0:T(8,128)S(1)}, u32[]{:S(2)}, u32[]{:S(2)}) collective-permute-start(f32[65,128]{1,0:T(8,128)S(1)} %bitcast.70), channel_id=1, source_target_pairs={{0,1},{1,0},{2,3},{3,2},{4,5},{5,4},{6,7},{7,6},{8,9},{9,8},{10,11... | collective-permute-start | bytes 99848 | tf_op jit(solution)/shard_map/ppermute | solution.py:18
  5.5 1.3 collective-permute-start.2
  6.8 3.0 %collective-permute-start = (f32[65,1,128]{2,1,0:T(1,128)S(1)}, f32[65,1,128]{2,1,0:T(1,128)S(1)}, u32[]{:S(2)}, u32[]{:S(2)}) collective-permute-start(f32[65,1,128]{2,1,0:T(1,128)S(1)} %get-tuple-element.33), channel_id=1, source_target_pairs={{0,2},{2,4},{4,6},{6,8},{8,10},{10,12},{12,14},{14,16},{16,18},{18... | collective-permute-start | bytes 99848 | tf_op jit(solution)/shard_map/ppermute | solution.py:29
  12.5 2.0 %collective-permute-start.3 = (f32[65,10,1]{0,2,1:T(1,128)S(1)}, f32[65,10,1]{0,2,1:T(1,128)S(1)}, u32[]{:S(2)}, u32[]{:S(2)}) collective-permute-start(f32[65,10,1]{0,2,1:T(1,128)S(1)} %copy.30), channel_id=1, source_target_pairs={{0,1},{1,0},{2,3},{3,2},{4,5},{5,4},{6,7},{7,6},{8,9},{9,8},{10,11... | collective-permute-start | bytes 7808 | tf_op jit(solution)/shard_map/ppermute | solution.py:29
  14.6 1.6 collective-permute-done.3
  17.8 2.2 %collective-permute-start.5 = (f32[1,1,128]{2,1,0:T(1,128)S(1)}, f32[1,1,128]{2,1,0:T(1,128)S(1)}, u32[]{:S(2)}, u32[]{:S(2)}) collective-permute-start(f32[1,1,128]{2,1,0:T(1,128)S(1)} %get-tuple-element.49), channel_id=1, source_target_pairs={{0,2},{2,4},{4,6},{6,8},{8,10},{10,12},{12,14},{14,16},{16,18},{18... | collective-permute-start | bytes 1544 | tf_op jit(solution)/shard_map/ppermute | solution.py:29
  19.9 1.9 %collective-permute-start.6 = (f32[1,128]{1,0:T(1,128)S(1)}, f32[1,128]{1,0:T(1,128)S(1)}, u32[]{:S(2)}, u32[]{:S(2)}) collective-permute-start(f32[1,128]{1,0:T(1,128)S(1)} %get-tuple-element.50), channel_id=1, source_target_pairs={{0,1},{1,0},{2,3},{3,2},{4,5},{5,4},{6,7},{7,6},{8,9},{9,8},{10,11... | collective-permute-start | bytes 1544 | tf_op jit(solution)/shard_map/ppermute | solution.py:18
  25.2 2.3 %collective-permute-done.7 = f32[1,1,128]{2,1,0:T(1,128)S(1)} collective-permute-done((f32[1,1,128]{2,1,0:T(1,128)S(1)}, f32[1,1,128]{2,1,0:T(1,128)S(1)}, u32[]{:S(2)}, u32[]{:S(2)}) %collective-permute-start.7) | collective-permute-done | bytes 544 | tf_op jit(solution)/shard_map/ppermute | solution.py:31
  28.2 1.5 collective-permute-start.9
  29.6 1.6 collective-permute-done.8
  32.6 5.5 %all-reduce.7 = (f32[]{:T(128)}, f32[]{:T(128)}) all-reduce(f32[]{:T(128)} %get-tuple-element.13, f32[]{:T(128)} %get-tuple-element.12), channel_id=1, replica_groups=mesh['blk'=16,'grp'=2] {'grp'}, use_global_device_ids=true, to_apply=%region_3.4 | all-reduce | flops 2 | bytes 16 | tf_op jit(solution)/shard_map/psum | solution.py:13
  38.1 32.3 %all-reduce.4 = (f32[]{:T(128)}, f32[]{:T(128)}) all-reduce(f32[]{:T(128)} %get-tuple-element.24, f32[]{:T(128)} %get-tuple-element.25), channel_id=1, replica_groups=mesh['blk'=16,'grp'=2] {'blk'}, use_global_device_ids=true, to_apply=%region_4.5 | all-reduce | flops 2 | bytes 16 | tf_op jit(solution)/shard_map/psum | solution.py:14
  71.8 1.6 collective-permute-start.11
  74.9 3.0 %collective-permute-start.10 = (f32[1,1,128]{2,1,0:T(1,128)S(1)}, f32[1,1,128]{2,1,0:T(1,128)S(1)}, u32[]{:S(2)}, u32[]{:S(2)}) collective-permute-start(f32[1,1,128]{2,1,0:T(1,128)S(1)} %get-tuple-element.46), channel_id=1, source_target_pairs={{0,2},{2,4},{4,6},{6,8},{8,10},{10,12},{12,14},{14,16},{16,18},{18... | collective-permute-start | bytes 1544 | tf_op jit(solution)/shard_map/ppermute | solution.py:29
  79.4 1.5 collective-permute-start.14
  80.9 1.6 collective-permute-done.13
  83.8 5.6 %all-reduce.6 = (f32[]{:T(128)}, f32[]{:T(128)}) all-reduce(f32[]{:T(128)} %get-tuple-element.11, f32[]{:T(128)} %get-tuple-element.10), channel_id=1, replica_groups=mesh['blk'=16,'grp'=2] {'grp'}, use_global_device_ids=true, to_apply=%region_9.10 | all-reduce | flops 2 | bytes 16 | tf_op jit(solution)/shard_map/psum | solution.py:13
  89.4 30.2 %all-reduce.3 = (f32[]{:T(128)}, f32[]{:T(128)}) all-reduce(f32[]{:T(128)} %get-tuple-element.22, f32[]{:T(128)} %get-tuple-element.23), channel_id=1, replica_groups=mesh['blk'=16,'grp'=2] {'blk'}, use_global_device_ids=true, to_apply=%region_10.11 | all-reduce | flops 2 | bytes 16 | tf_op jit(solution)/shard_map/psum | solution.py:14
  124.2 1.6 collective-permute-start.16
  127.9 3.0 %collective-permute-start.15 = (f32[1,1,128]{2,1,0:T(1,128)S(1)}, f32[1,1,128]{2,1,0:T(1,128)S(1)}, u32[]{:S(2)}, u32[]{:S(2)}) collective-permute-start(f32[1,1,128]{2,1,0:T(1,128)S(1)} %get-tuple-element.43), channel_id=1, source_target_pairs={{0,2},{2,4},{4,6},{6,8},{8,10},{10,12},{12,14},{14,16},{16,18},{18... | collective-permute-start | bytes 1544 | tf_op jit(solution)/shard_map/ppermute | solution.py:29
  132.4 1.5 collective-permute-start.19
  133.9 1.7 collective-permute-done.18
  136.8 5.5 %all-reduce.5 = (f32[]{:T(128)}, f32[]{:T(128)}) all-reduce(f32[]{:T(128)} %get-tuple-element.9, f32[]{:T(128)} %get-tuple-element.8), channel_id=1, replica_groups=mesh['blk'=16,'grp'=2] {'grp'}, use_global_device_ids=true, to_apply=%region_15.16 | all-reduce | flops 2 | bytes 16 | tf_op jit(solution)/shard_map/psum | solution.py:13
  142.3 30.1 %all-reduce.2 = (f32[]{:T(128)}, f32[]{:T(128)}) all-reduce(f32[]{:T(128)} %get-tuple-element.20, f32[]{:T(128)} %get-tuple-element.21), channel_id=1, replica_groups=mesh['blk'=16,'grp'=2] {'blk'}, use_global_device_ids=true, to_apply=%region_16.17 | all-reduce | flops 2 | bytes 16 | tf_op jit(solution)/shard_map/psum | solution.py:14
  (89 shorter events, 20.9 us)
Async XLA Ops:
  2.5 7.4 %collective-permute-start.1 = (f32[65,128]{1,0:T(8,128)S(1)}, f32[65,128]{1,0:T(8,128)S(1)}, u32[]{:S(2)}, u32[]{:S(2)}) collective-permute-start(f32[65,128]{1,0:T(8,128)S(1)} %bitcast.70), channel_id=1, source_target_pairs={{0,1},{1,0},{2,3},{3,2},{4,5},{5,4},{6,7},{7,6},{8,9},{9,8},{10,11... | collective-permute-start | bytes 99848 | tf_op jit(solution)/shard_map/ppermute | solution.py:18
  5.5 4.4 %collective-permute-start.2 = (f32[65,1,128]{2,0,1:T(8,128)S(1)}, f32[65,1,128]{2,0,1:T(8,128)S(1)}, u32[]{:S(2)}, u32[]{:S(2)}) collective-permute-start(f32[65,1,128]{2,0,1:T(8,128)S(1)} %copy.46), channel_id=1, source_target_pairs={{2,0},{4,2},{6,4},{8,6},{10,8},{12,10},{14,12},{16,14},{18,16},{20... | collective-permute-start | bytes 99848 | tf_op jit(solution)/shard_map/ppermute | solution.py:31
  6.8 3.9 %collective-permute-start = (f32[65,1,128]{2,1,0:T(1,128)S(1)}, f32[65,1,128]{2,1,0:T(1,128)S(1)}, u32[]{:S(2)}, u32[]{:S(2)}) collective-permute-start(f32[65,1,128]{2,1,0:T(1,128)S(1)} %get-tuple-element.33), channel_id=1, source_target_pairs={{0,2},{2,4},{4,6},{6,8},{8,10},{10,12},{12,14},{14,16},{16,18},{18... | collective-permute-start | bytes 99848 | tf_op jit(solution)/shard_map/ppermute | solution.py:29
  12.0 2.5 %copy-start = (f32[2,16,8,128]{3,2,1,0:T(8,128)S(1)}, f32[2,16,8,128]{3,2,1,0:T(8,128)}, u32[]{:S(2)}) copy-start(f32[2,16,8,128]{3,2,1,0:T(8,128)} %param.5) | copy-start | bytes 393220
  12.0 2.5 %copy-start.1 = (f32[2,16,8,128]{3,2,1,0:T(8,128)S(1)}, f32[2,16,8,128]{3,2,1,0:T(8,128)}, u32[]{:S(2)}) copy-start(f32[2,16,8,128]{3,2,1,0:T(8,128)} %param.4) | copy-start | bytes 393220
  12.4 4.1 %collective-permute-start.4 = (f32[65,10,1]{0,2,1:T(1,128)S(1)}, f32[65,10,1]{0,2,1:T(1,128)S(1)}, u32[]{:S(2)}, u32[]{:S(2)}) collective-permute-start(f32[65,10,1]{0,2,1:T(1,128)S(1)} %copy.31), channel_id=1, source_target_pairs={{1,0},{0,1},{3,2},{2,3},{5,4},{4,5},{7,6},{6,7},{9,8},{8,9},{11,10... | collective-permute-start | bytes 7808 | tf_op jit(solution)/shard_map/ppermute | solution.py:31
  12.5 3.7 %collective-permute-start.3 = (f32[65,10,1]{0,2,1:T(1,128)S(1)}, f32[65,10,1]{0,2,1:T(1,128)S(1)}, u32[]{:S(2)}, u32[]{:S(2)}) collective-permute-start(f32[65,10,1]{0,2,1:T(1,128)S(1)} %copy.30), channel_id=1, source_target_pairs={{0,1},{1,0},{2,3},{3,2},{4,5},{5,4},{6,7},{7,6},{8,9},{9,8},{10,11... | collective-permute-start | bytes 7808 | tf_op jit(solution)/shard_map/ppermute | solution.py:29
  17.8 9.8 %collective-permute-start.5 = (f32[1,1,128]{2,1,0:T(1,128)S(1)}, f32[1,1,128]{2,1,0:T(1,128)S(1)}, u32[]{:S(2)}, u32[]{:S(2)}) collective-permute-start(f32[1,1,128]{2,1,0:T(1,128)S(1)} %get-tuple-element.49), channel_id=1, source_target_pairs={{0,2},{2,4},{4,6},{6,8},{8,10},{10,12},{12,14},{14,16},{16,18},{18... | collective-permute-start | bytes 1544 | tf_op jit(solution)/shard_map/ppermute | solution.py:29
  19.9 5.2 %collective-permute-start.6 = (f32[1,128]{1,0:T(1,128)S(1)}, f32[1,128]{1,0:T(1,128)S(1)}, u32[]{:S(2)}, u32[]{:S(2)}) collective-permute-start(f32[1,128]{1,0:T(1,128)S(1)} %get-tuple-element.50), channel_id=1, source_target_pairs={{0,1},{1,0},{2,3},{3,2},{4,5},{5,4},{6,7},{7,6},{8,9},{9,8},{10,11... | collective-permute-start | bytes 1544 | tf_op jit(solution)/shard_map/ppermute | solution.py:18
  21.8 5.7 %collective-permute-start.7 = (f32[1,1,128]{2,1,0:T(1,128)S(1)}, f32[1,1,128]{2,1,0:T(1,128)S(1)}, u32[]{:S(2)}, u32[]{:S(2)}) collective-permute-start(f32[1,1,128]{2,1,0:T(1,128)S(1)} %get-tuple-element.51), channel_id=1, source_target_pairs={{2,0},{4,2},{6,4},{8,6},{10,8},{12,10},{14,12},{16,14},{18,16},{20... | collective-permute-start | bytes 1544 | tf_op jit(solution)/shard_map/ppermute | solution.py:31
  24.3 0.7 copy-start.2
  27.6 3.7 %collective-permute-start.8 = (f32[1,10,1]{2,1,0:T(8,128)S(1)}, f32[1,10,1]{2,1,0:T(8,128)S(1)}, u32[]{:S(2)}, u32[]{:S(2)}) collective-permute-start(f32[1,10,1]{2,1,0:T(8,128)S(1)} %get-tuple-element.39), channel_id=1, source_target_pairs={{0,1},{1,0},{2,3},{3,2},{4,5},{5,4},{6,7},{7,6},{8,9},{9,8},{10,11... | collective-permute-start | bytes 128 | tf_op jit(solution)/shard_map/ppermute | solution.py:29
  28.2 3.7 %collective-permute-start.9 = (f32[1,10,1]{2,1,0:T(8,128)S(1)}, f32[1,10,1]{2,1,0:T(8,128)S(1)}, u32[]{:S(2)}, u32[]{:S(2)}) collective-permute-start(f32[1,10,1]{2,1,0:T(8,128)S(1)} %get-tuple-element.40), channel_id=1, source_target_pairs={{1,0},{0,1},{3,2},{2,3},{5,4},{4,5},{7,6},{6,7},{9,8},{8,9},{11,10... | collective-permute-start | bytes 128 | tf_op jit(solution)/shard_map/ppermute | solution.py:31
  71.8 6.1 %collective-permute-start.11 = (f32[1,128]{1,0:T(1,128)S(1)}, f32[1,128]{1,0:T(1,128)S(1)}, u32[]{:S(2)}, u32[]{:S(2)}) collective-permute-start(f32[1,128]{1,0:T(1,128)S(1)} %get-tuple-element.47), channel_id=1, source_target_pairs={{0,1},{1,0},{2,3},{3,2},{4,5},{5,4},{6,7},{7,6},{8,9},{9,8},{10,11... | collective-permute-start | bytes 1544 | tf_op jit(solution)/shard_map/ppermute | solution.py:18
  73.4 4.7 %collective-permute-start.12 = (f32[1,1,128]{2,1,0:T(1,128)S(1)}, f32[1,1,128]{2,1,0:T(1,128)S(1)}, u32[]{:S(2)}, u32[]{:S(2)}) collective-permute-start(f32[1,1,128]{2,1,0:T(1,128)S(1)} %get-tuple-element.48), channel_id=1, source_target_pairs={{2,0},{4,2},{6,4},{8,6},{10,8},{12,10},{14,12},{16,14},{18,16},{20... | collective-permute-start | bytes 1544 | tf_op jit(solution)/shard_map/ppermute | solution.py:31
  74.9 3.8 %collective-permute-start.10 = (f32[1,1,128]{2,1,0:T(1,128)S(1)}, f32[1,1,128]{2,1,0:T(1,128)S(1)}, u32[]{:S(2)}, u32[]{:S(2)}) collective-permute-start(f32[1,1,128]{2,1,0:T(1,128)S(1)} %get-tuple-element.46), channel_id=1, source_target_pairs={{0,2},{2,4},{4,6},{6,8},{8,10},{10,12},{12,14},{14,16},{16,18},{18... | collective-permute-start | bytes 1544 | tf_op jit(solution)/shard_map/ppermute | solution.py:29
  78.8 3.7 %collective-permute-start.13 = (f32[1,10,1]{2,1,0:T(8,128)S(1)}, f32[1,10,1]{2,1,0:T(8,128)S(1)}, u32[]{:S(2)}, u32[]{:S(2)}) collective-permute-start(f32[1,10,1]{2,1,0:T(8,128)S(1)} %get-tuple-element.37), channel_id=1, source_target_pairs={{0,1},{1,0},{2,3},{3,2},{4,5},{5,4},{6,7},{7,6},{8,9},{9,8},{10,11... | collective-permute-start | bytes 128 | tf_op jit(solution)/shard_map/ppermute | solution.py:29
  79.4 3.7 %collective-permute-start.14 = (f32[1,10,1]{2,1,0:T(8,128)S(1)}, f32[1,10,1]{2,1,0:T(8,128)S(1)}, u32[]{:S(2)}, u32[]{:S(2)}) collective-permute-start(f32[1,10,1]{2,1,0:T(8,128)S(1)} %get-tuple-element.38), channel_id=1, source_target_pairs={{1,0},{0,1},{3,2},{2,3},{5,4},{4,5},{7,6},{6,7},{9,8},{8,9},{11,10... | collective-permute-start | bytes 128 | tf_op jit(solution)/shard_map/ppermute | solution.py:31
  124.2 6.8 %collective-permute-start.16 = (f32[1,128]{1,0:T(1,128)S(1)}, f32[1,128]{1,0:T(1,128)S(1)}, u32[]{:S(2)}, u32[]{:S(2)}) collective-permute-start(f32[1,128]{1,0:T(1,128)S(1)} %get-tuple-element.44), channel_id=1, source_target_pairs={{0,1},{1,0},{2,3},{3,2},{4,5},{5,4},{6,7},{7,6},{8,9},{9,8},{10,11... | collective-permute-start | bytes 1544 | tf_op jit(solution)/shard_map/ppermute | solution.py:18
  125.8 5.3 %collective-permute-start.17 = (f32[1,1,128]{2,1,0:T(1,128)S(1)}, f32[1,1,128]{2,1,0:T(1,128)S(1)}, u32[]{:S(2)}, u32[]{:S(2)}) collective-permute-start(f32[1,1,128]{2,1,0:T(1,128)S(1)} %get-tuple-element.45), channel_id=1, source_target_pairs={{2,0},{4,2},{6,4},{8,6},{10,8},{12,10},{14,12},{16,14},{18,16},{20... | collective-permute-start | bytes 1544 | tf_op jit(solution)/shard_map/ppermute | solution.py:31
  127.9 3.8 %collective-permute-start.15 = (f32[1,1,128]{2,1,0:T(1,128)S(1)}, f32[1,1,128]{2,1,0:T(1,128)S(1)}, u32[]{:S(2)}, u32[]{:S(2)}) collective-permute-start(f32[1,1,128]{2,1,0:T(1,128)S(1)} %get-tuple-element.43), channel_id=1, source_target_pairs={{0,2},{2,4},{4,6},{6,8},{8,10},{10,12},{12,14},{14,16},{16,18},{18... | collective-permute-start | bytes 1544 | tf_op jit(solution)/shard_map/ppermute | solution.py:29
  131.8 3.7 %collective-permute-start.18 = (f32[1,10,1]{2,1,0:T(8,128)S(1)}, f32[1,10,1]{2,1,0:T(8,128)S(1)}, u32[]{:S(2)}, u32[]{:S(2)}) collective-permute-start(f32[1,10,1]{2,1,0:T(8,128)S(1)} %get-tuple-element.35), channel_id=1, source_target_pairs={{0,1},{1,0},{2,3},{3,2},{4,5},{5,4},{6,7},{7,6},{8,9},{9,8},{10,11... | collective-permute-start | bytes 128 | tf_op jit(solution)/shard_map/ppermute | solution.py:29
  132.4 3.7 %collective-permute-start.19 = (f32[1,10,1]{2,1,0:T(8,128)S(1)}, f32[1,10,1]{2,1,0:T(8,128)S(1)}, u32[]{:S(2)}, u32[]{:S(2)}) collective-permute-start(f32[1,10,1]{2,1,0:T(8,128)S(1)} %get-tuple-element.36), channel_id=1, source_target_pairs={{1,0},{0,1},{3,2},{2,3},{5,4},{4,5},{7,6},{6,7},{9,8},{8,9},{11,10... | collective-permute-start | bytes 128 | tf_op jit(solution)/shard_map/ppermute | solution.py:31
